TPU v7x, 32 devices: a whole 2x2x4 slice. The times are simulated.
32 devices in a mesh: row: 4 (over z), col: 8 (over y, x, core).
Axes of the slice: x: 2, y: 2, z: 4, core: 2. Of those that a mesh axis runs over, the one named last changes fastest.
Arguments:
- slab_left: bfloat16 [16, 8, 2048, 32], P('row', 'col'), may hold values from -6 to 6
- slab_right: bfloat16 [16, 8, 2048, 32], P('row', 'col'), may hold values from -1 to 1
- slab_ranks: int32 [16, 8], P('row', 'col'), may hold values from 20 to 32
- panel_left: bfloat16 [16, 2048, 32], P('row', 'col'), may hold values from -6 to 6
- panel_right: bfloat16 [16, 2048, 32], P('row', 'col'), may hold values from -0.125 to 0.125
- panel_ranks: int32 [16], P('row'), may hold values from 20 to 32
- inverse_factor: bfloat16 [2048, 2048], P(None, 'col'), may hold values from -2 to 2, as said below
- sketch: bfloat16 [2048, 32], replicated, may hold values from -6 to 6
Outputs:
- new_left: bfloat16 [16, 8, 2048, 32], P('row', 'col')
- new_right: bfloat16 [16, 8, 2048, 32], P('row', 'col')
Inputs may be any that keep to these rules, and one draw needn't show every extreme that they name: `slab_ranks`: number of live columns of a slab tile's factors; columns from that index on are padding. `panel_ranks`: number of live columns of a panel tile's factors; columns from that index on are padding. `inverse_factor`: lower triangular: entries above the diagonal are zero, diagonal entries positive.
All inputs are finite; a program needn't handle non-finite values.
Results may differ from a plain program's by a relative error of at most 0.0073.
Values may be sent and summed in bfloat16 or wider, within the bound.
No kernel may reach another device: no remote copies, remote signals or barrier semaphores. Data moves between devices by JAX's collectives and lax.ppermute only.
A program may use at most 64 MiB of HBM per device.

v0:
```python
import math
import jax
import jax.numpy as jnp
from jax import lax
from jax.sharding import PartitionSpec as P

highest = lax.Precision.HIGHEST
stacked_precision = lax.Precision.HIGH
shift_rate = 0.01
tiny_shift = 1e-06
factor_scale = 0.5


def spread(block, axis, owner):
    block = jnp.where(lax.axis_index(axis) == owner, block, jnp.zeros_like(block))
    return lax.psum(block, axis)


def product(first_matrix, second_matrix):
    return jnp.matmul(first_matrix, second_matrix, precision=highest)


def stacked_product(first_matrix, second_matrix):
    return jnp.matmul(first_matrix, second_matrix, precision=stacked_precision)


def flipped(matrix):
    return jnp.swapaxes(matrix, -1, -2)


def orthonormal(vectors):
    gram_matrix = product(flipped(vectors), vectors)
    shift_value = (
        shift_rate * jnp.trace(gram_matrix, axis1=-2, axis2=-1) / gram_matrix.shape[-1] + tiny_shift
    )
    identity = jnp.eye(gram_matrix.shape[-1], dtype=gram_matrix.dtype)
    lower_factor = jnp.linalg.cholesky(gram_matrix + shift_value[..., None, None] * identity)
    solved_rows = lax.linalg.triangular_solve(
        lower_factor, flipped(vectors), left_side=True, lower=True
    )
    return flipped(solved_rows)


def recompress(slab_factor, masked_right, row_factor, core_block, column_factor, sketch_float):
    target_shape = core_block.shape[:2] + slab_factor.shape[2:]
    column_wide = jnp.broadcast_to(column_factor[None], target_shape)
    row_core = product(row_factor, core_block)
    column_core = product(column_wide, flipped(core_block))
    forward_left = jnp.concatenate([slab_factor.astype(jnp.float32), -row_core], axis=-1)
    forward_right = jnp.concatenate([masked_right.astype(jnp.float32), column_wide], axis=-1)
    backward_left = jnp.concatenate([masked_right.astype(jnp.float32), -column_core], axis=-1)
    backward_right = jnp.concatenate([slab_factor.astype(jnp.float32), row_factor], axis=-1)

    def forward(vectors):
        return stacked_product(forward_left, stacked_product(flipped(forward_right), vectors))

    def backward(vectors):
        return stacked_product(backward_left, stacked_product(flipped(backward_right), vectors))

    basis_now = orthonormal(forward(sketch_float))
    basis_now = orthonormal(forward(backward(basis_now)))
    projected = backward(basis_now)
    factor_size = factor_scale * math.sqrt(slab_factor.shape[-2])
    return (basis_now * factor_size, projected / factor_size)


def shards(
    slab_left, slab_right, slab_ranks, panel_left, panel_right, panel_ranks, inverse_factor, sketch
):
    rows_total = lax.axis_size("row")
    cols_total = lax.axis_size("col")
    my_row = lax.axis_index("row")
    my_col = lax.axis_index("col")
    tile_rows, piece_rows, rank_width = panel_left.shape
    column_tiles = slab_left.shape[1]
    tile_order = inverse_factor.shape[0]
    panel_keep = jnp.arange(rank_width, dtype=jnp.int32)[None, :] < panel_ranks[:, None]
    masked_panel = jnp.where(panel_keep[:, None, :], panel_right, jnp.zeros((), jnp.bfloat16))
    flat_right = jnp.swapaxes(masked_panel, 0, 1).reshape(piece_rows, tile_rows * rank_width)
    flat_left = jnp.swapaxes(panel_left, 0, 1).reshape(piece_rows, tile_rows * rank_width)
    solved_part = lax.psum_scatter(
        jnp.dot(inverse_factor, flat_right, preferred_element_type=jnp.float32),
        "col",
        scatter_dimension=0,
        tiled=True,
    ).astype(jnp.bfloat16)
    full_left, full_solved = (
        lax.all_gather(flat_left, "col", axis=0, tiled=True),
        lax.all_gather(solved_part, "col", axis=0, tiled=True),
    )
    full_left = full_left.reshape(tile_order, tile_rows, rank_width)
    full_solved = full_solved.reshape(tile_order, tile_rows, rank_width)
    first_pick = my_col // rows_total
    position = first_pick + 0
    picked_left = lax.dynamic_slice_in_dim(full_left, position, 1, 1)
    picked_solved = lax.dynamic_slice_in_dim(full_solved, position, 1, 1)
    send_left = picked_left.reshape(tile_order, column_tiles * rank_width)
    send_solved = picked_solved.reshape(tile_order, column_tiles * rank_width)
    root_row = my_col % rows_total
    column_left, column_solved = (
        spread(send_left, "row", root_row),
        spread(send_solved, "row", root_row),
    )
    row_factor = jnp.swapaxes(full_left, 0, 1)[:, None]
    row_solved = jnp.swapaxes(full_solved, 0, 1)
    column_factor = jnp.swapaxes(column_left.reshape(tile_order, column_tiles, rank_width), 0, 1)
    column_three = jnp.swapaxes(column_solved.reshape(tile_order, column_tiles, rank_width), 0, 1)
    core_block = jnp.einsum(
        "tbr,sbq->tsrq", row_solved, column_three, preferred_element_type=jnp.float32
    )
    slab_keep = jnp.arange(rank_width, dtype=jnp.int32) < slab_ranks[..., None]
    masked_right = jnp.where(slab_keep[:, :, None, :], slab_right, jnp.zeros((), jnp.bfloat16))
    fresh_left, fresh_right = recompress(
        slab_left, masked_right, row_factor, core_block, column_factor, sketch.astype(jnp.float32)
    )
    row_ids = jnp.arange(tile_rows, dtype=jnp.int32) * rows_total + my_row
    col_ids = jnp.arange(column_tiles, dtype=jnp.int32) * cols_total + my_col
    live_tile = (row_ids[:, None] > col_ids[None, :])[:, :, None, None]
    return (
        jnp.where(live_tile, fresh_left, 0.0).astype(jnp.bfloat16),
        jnp.where(live_tile, fresh_right, 0.0).astype(jnp.bfloat16),
    )


def solution(mesh):
    placed = (
        P("row", "col", None, None),
        P("row", "col", None, None),
        P("row", "col"),
        P("row", "col", None),
        P("row", "col", None),
        P("row"),
        P(None, "col"),
        P(),
    )
    return jax.shard_map(
        shards,
        mesh=mesh,
        in_specs=placed,
        out_specs=(P("row", "col", None, None), P("row", "col", None, None)),
        check_vma=False,
    )
```

profile of v0, /device:TPU:0, one launch (start us, length us, event | category | flops | bytes accessed | tf_op | source)
XLA Modules:
  0.0 172.6 jit_solution(16440172351026109829)
XLA Ops:
  7.2 0.0 copy-start
  7.2 0.0 reduce-scatter.2.cloned.1.call-start
  7.2 0.8 iota_compare_fusion.4
  8.0 0.9 broadcast_select_fusion
  9.0 1.4 convolution_bitcast_fusion.1
  10.4 0.0 reduce-scatter.2.cloned.1.call-update
  10.4 0.0 all-reduce.3.cloned.1.call-start
  10.6 0.7 copy-done.18
  11.3 12.4 %all_gather.7 = bf16[2048,128]{0,1:T(8,128)(2,1)S(1)} all-gather(bf16[256,128]{0,1:T(8,128)(2,1)S(1)} %bitcast.193), channel_id=1, replica_groups=mesh['row'=4,'col'=8] {'col'}, dimensions={0}, use_global_device_ids=true | all-gather | bytes 589824 | tf_op jit(solution)/shard_map/all_gather | solution.py:88
  23.7 0.1 iota_compare_fusion.3
  23.7 0.7 select_bitcast_fusion
  24.4 0.1 copy-done.11
  24.5 0.1 bitcast_convert_fusion
  24.6 0.4 copy-done.16
  24.9 0.1 fusion.35
  25.1 24.9 %reduce-scatter.2.cloned.1.call-done = f32[256,128]{0,1:T(8,128)} async-done(((f32[2048,128]{0,1:T(8,128)}), f32[256,128]{0,1:T(8,128)}) %reduce-scatter.2.cloned.1.call-update) | async-done | bytes 131088 | tf_op jit(solution)/shard_map/reduce_scatter | solution.py:81
  49.9 0.9 convert_element_type.45
  50.8 10.9 %all_gather.6 = bf16[2048,128]{0,1:T(8,128)(2,1)S(1)} all-gather(bf16[256,128]{0,1:T(8,128)(2,1)S(1)} %convert_element_type.45), channel_id=1, replica_groups=mesh['row'=4,'col'=8] {'col'}, dimensions={0}, use_global_device_ids=true | all-gather | bytes 589824 | tf_op jit(solution)/shard_map/all_gather | solution.py:89
  61.7 0.8 copy-done.13
  62.5 0.7 select_bitcast_fusion.1
  63.2 0.0 all-reduce.3.cloned.1.call-update
  63.2 0.1 copy.30
  63.3 2.1 %convert.1 = f32[4,1,2048,32]{2,3,0,1:T(8,128)} convert(bf16[4,1,2048,32]{2,3,0,1:T(8,128)(2,1)} %bitcast.188) | non-fusion elementwise | flops 262144 | bytes 1572864 | tf_op jit(solution)/shard_map/convert_element_type | solution.py:52
  65.5 33.6 %all-reduce.3.cloned.1.call-done = (bf16[2048,32]{0,1:T(8,128)(2,1)}, bf16[2048,32]{0,1:T(8,128)(2,1)}) async-done(((bf16[2048,32]{0,1:T(8,128)(2,1)}, bf16[2048,32]{0,1:T(8,128)(2,1)}), (bf16[2048,32]{0,1:T(8,128)(2,1)}, bf16[2048,32]{0,1:T(8,128)(2,1)})) %all-reduce.3.cloned.1.call-update) | async-done | bytes 262160 | tf_op jit(solution)/shard_map/psum | solution.py:16
  99.0 1.7 fusion.38
  100.7 0.0 copy-done.12
  100.7 0.6 fusion.2
  101.3 1.7 fusion.1
  103.0 0.1 broadcast_in_dim.97
  103.1 1.0 copy-done.9
  104.1 1.1 fusion.11
  105.2 0.0 copy-done.5
  105.2 0.6 fusion.19
  105.9 1.2 select_reduce_fusion.1
  107.0 0.1 copy.31
  107.1 0.1 fusion.55
  107.2 0.1 copy.32
  107.3 0.1 fusion.42
  107.4 11.9 %custom-call.8 = f32[4,1,32,32]{3,2,1,0:T(8,128)S(1)} custom-call(f32[4,1,32,32]{3,2,1,0:T(8,128)S(1)} %fusion.42), custom_call_target="Cholesky" | custom-call | tf_op jit(solution)/shard_map/jit(cholesky)/cholesky | solution.py:37
  119.3 0.1 compare_reduce_fusion.1
  119.5 0.1 fusion.54
  119.5 9.8 %custom-call.9 = f32[4,1,1,32,32]{3,4,2,1,0:T(8,128)S(1)} custom-call(f32[4,1,1,32,32]{4,3,2,1,0:T(8,128)S(1)} %fusion.54), custom_call_target="InvertDiagBlocksLowerTriangular" | custom-call | tf_op jit(solution)/shard_map/triangular_solve/custom-call.0 | solution.py:38
  129.4 2.4 %convolution_bitcast_fusion = f32[4,2048,32]{1,2,0:T(8,128)S(1)} fusion(f32[4,2048,32]{1,2,0:T(8,128)} %copy-done.2, f32[4,1,1,32,32]{3,4,2,1,0:T(8,128)S(1)} %custom-call.9), kind=kOutput, calls=%fused_computation.6 | convolution fusion | flops 100663296 | bytes 2113536 | tf_op jit(solution)/shard_map/triangular_solve/dot.5 | solution.py:38
  131.8 1.0 fusion.15
  132.8 0.2 copy-done.7
  133.0 0.7 fusion.22
  133.7 0.5 copy-done.10
  134.2 1.0 fusion.9
  135.2 0.2 copy-done.6
  135.4 0.6 fusion.17
  136.1 1.2 select_reduce_fusion
  137.3 0.1 copy.37
  137.4 0.1 fusion.56
  137.5 0.1 copy.38
  137.5 0.1 fusion.40
  137.6 11.7 %custom-call.10 = f32[4,1,32,32]{3,2,1,0:T(8,128)S(1)} custom-call(f32[4,1,32,32]{3,2,1,0:T(8,128)S(1)} %fusion.40), custom_call_target="Cholesky" | custom-call | tf_op jit(solution)/shard_map/jit(cholesky)/cholesky | solution.py:37
  149.4 0.1 compare_reduce_fusion
  149.5 0.1 fusion.49
  149.6 9.8 %custom-call.11 = f32[4,1,1,32,32]{3,4,2,1,0:T(8,128)S(1)} custom-call(f32[4,1,1,32,32]{4,3,2,1,0:T(8,128)S(1)} %fusion.49), custom_call_target="InvertDiagBlocksLowerTriangular" | custom-call | tf_op jit(solution)/shard_map/triangular_solve/custom-call.0 | solution.py:38
  159.4 2.4 %fusion.24 = f32[4,32,2048]{2,1,0:T(8,128)S(1)} fusion(f32[4,2048,32]{1,2,0:T(8,128)} %copy-done.1, f32[4,1,1,32,32]{3,4,2,1,0:T(8,128)S(1)} %custom-call.11), kind=kOutput, calls=%fused_computation.25 | convolution fusion | flops 100663296 | bytes 2113536 | tf_op jit(solution)/shard_map/triangular_solve/dot.5 | solution.py:38
  161.8 1.0 fusion.13
  162.9 1.0 fusion.34
  163.8 0.4 copy-done.8
  164.3 1.4 fusion.4
  (37 shorter events, 0.2 us)
Async XLA Ops:
  7.2 1.8 %copy-start = (bf16[2048,256]{1,0:T(8,128)(2,1)S(1)}, bf16[2048,256]{1,0:T(8,128)(2,1)}, u32[]{:S(2)}) copy-start(bf16[2048,256]{1,0:T(8,128)(2,1)} %param.17) | copy-start | bytes 3145732
  7.2 42.8 %reduce-scatter.2.cloned.1.call-start = ((), (), s32[]{:S(2)}) async-start(), calls=%async_computation.1 | async-start | bytes 1179648 | tf_op jit(solution)/shard_map/reduce_scatter | solution.py:81
  10.4 0.8 copy-start.18
  10.4 13.2 %copy-start.19 = (s32[4,1]{0,1:T(1,128)S(1)}, s32[4,1]{0,1:T(1,128)}, u32[]{:S(2)}) copy-start(s32[4,1]{0,1:T(1,128)} %param.13) | copy-start | bytes 52
  10.4 14.1 %copy-start.14 = (bf16[4,1,2048,32]{2,3,1,0:T(8,128)(2,1)S(1)}, bf16[4,1,2048,32]{2,3,1,0:T(8,128)(2,1)}, u32[]{:S(2)}) copy-start(bf16[4,1,2048,32]{2,3,1,0:T(8,128)(2,1)} %param.11) | copy-start | bytes 1572868
  10.4 88.6 %all-reduce.3.cloned.1.call-start = ((), (), s32[]{:S(2)}) async-start(), calls=%async_computation.2 | async-start | bytes 524288 | tf_op jit(solution)/shard_map/psum | solution.py:16
  23.6 0.8 copy-start.11
  23.6 1.3 copy-start.16
  61.7 0.8 copy-start.13
  99.0 1.7 copy-start.12
  99.0 2.3 %copy-start.15 = (bf16[2048,32]{0,1:T(8,128)(2,1)S(1)}, bf16[2048,32]{0,1:T(8,128)(2,1)}, u32[]{:S(2)}) copy-start(bf16[2048,32]{0,1:T(8,128)(2,1)} %get-tuple-element.8) | copy-start | bytes 393220
  101.3 3.9 %copy-start.5 = (f32[4,1,2048,32]{2,3,0,1:T(8,128)}, f32[4,1,2048,32]{2,3,0,1:T(8,128)S(1)}, u32[]{:S(2)}) copy-start(f32[4,1,2048,32]{2,3,0,1:T(8,128)S(1)} %fusion.2) | copy-start | bytes 3145732
  101.3 2.8 %copy-start.17 = (bf16[2048,32]{0,1:T(8,128)(2,1)S(1)}, bf16[2048,32]{0,1:T(8,128)(2,1)}, u32[]{:S(2)}) copy-start(bf16[2048,32]{0,1:T(8,128)(2,1)} %param.18) | copy-start | bytes 393220
  103.1 1.0 copy-start.9
  105.8 1.2 copy-start.2
  129.4 2.4 %copy-start.3 = (f32[4,1,2048,32]{2,3,0,1:T(8,128)S(1)}, f32[4,1,2048,32]{2,3,0,1:T(8,128)}, u32[]{:S(2)}) copy-start(f32[4,1,2048,32]{2,3,0,1:T(8,128)} %convert.1) | copy-start | bytes 3145732
  131.8 1.2 copy-start.7
  133.0 1.2 copy-start.10
  134.2 1.2 copy-start.6
  136.1 1.2 copy-start.1
  159.4 2.4 %copy-start.4 = (f32[4,1,2048,32]{2,3,0,1:T(8,128)S(1)}, f32[4,1,2048,32]{2,3,0,1:T(8,128)}, u32[]{:S(2)}) copy-start(f32[4,1,2048,32]{2,3,0,1:T(8,128)} %convert.1) | copy-start | bytes 3145732
  162.8 1.4 copy-start.8
Sparse Core Ops, SparseCore 0:
  11.2 38.7 reduce-scatter.1
  63.3 35.6 all-reduce.2
where the time goes:
time: 173 us
  waiting for transfers between devices  58.5 us (34%)
  other arithmetic  51.5 us (30%)
  blocking collectives  23.3 us (13%)
  matrix products  20 us (12%)
  between operations  14.4 us (8%)
  local copies, waits for them, and re-layouts  4.88 us (3%)
    psum x1, waiting for transfers between devices, spread(): return lax.psum(block, axis)  33.6 us
    reduce_scatter x1, waiting for transfers between devices, shards(): lax.psum_scatter(jnp.dot(inverse_factor, flat_right, preferred_element_ty...  24.9 us
    another operation x7, other arithmetic, orthonormal(): jnp.linalg.cholesky(gram_matrix + shift_value[..., None, None] * identity)  23.9 us
    another operation x5, other arithmetic, orthonormal(): lax.linalg.triangular_solve(lower_factor, flipped(vectors), left_side=Tru...  19.9 us
    all_gather x1, blocking collectives, shards(): lax.all_gather(flat_left, 'col', axis=0, tiled=True)  12.4 us
    all_gather x1, blocking collectives, shards(): lax.all_gather(solved_part, 'col', axis=0, tiled=True)  10.9 us
    dot_general x8, matrix products, stacked_product(): return jnp.matmul(first_matrix, second_matrix, precision=stacked_precision)  7.52 us
    another operation x2, matrix products, orthonormal(): lax.linalg.triangular_solve(lower_factor, flipped(vectors), left_side=Tru...  4.75 us
  transfers between devices with their start and end apart: 2, of which 2 were waited for; matrix products, arithmetic and copies ran while one was open for 2% of the time, Pallas kernels for 0%

commit v1 on v0

--- a/solution.py
+++ b/solution.py
@@ -11,9 +11,13 @@
 factor_scale = 0.5
 
 
+def loops_treat(mat, bus_axis):
+    return jnp.sum(jax.lax.all_gather(mat, axis_name=bus_axis), axis=0)
+
+
 def spread(block, axis, owner):
     block = jnp.where(lax.axis_index(axis) == owner, block, jnp.zeros_like(block))
-    return lax.psum(block, axis)
+    return loops_treat(block, axis)
 
 
 def product(first_matrix, second_matrix):

time: 173 us -> 155 us (0.90)
  waiting for transfers between devices: 58.5 us -> 5.15 us
  blocking collectives: 23.3 us -> 56.2 us
  local copies, waits for them, and re-layouts: 4.88 us -> 7.38 us
    psum x1 -> x0, waiting for transfers between devices: 33.6 us -> none  [spread(): return lax.psum(block, axis)]
    all_gather x0 -> x2, blocking collectives: none -> 32.9 us  [loops_treat(): return jnp.sum(jax.lax.all_gather(mat, axis_name=bus_axis), axis=0)]
    reduce_scatter x1, waiting for transfers between devices: 24.9 us -> 5.13 us  [shards(): lax.psum_scatter(jnp.dot(inverse_factor, flat_right, preferred_element_ty...]
    all_gather x0 -> x2, local copies, waits for them, and re-layouts: none -> 2.62 us  [loops_treat(): return jnp.sum(jax.lax.all_gather(mat, axis_name=bus_axis), axis=0)]
    reduce_sum x0 -> x2, other arithmetic: none -> 2.36 us  [loops_treat(): return jnp.sum(jax.lax.all_gather(mat, axis_name=bus_axis), axis=0)]
    unnamed x40 -> x38, local copies, waits for them, and re-layouts: 4.37 us -> 4.25 us
  transfers between devices with their start and end apart: 2 -> 1, of which waited for: 2 -> 1; matrix products, arithmetic and copies ran while one was open for 2% -> 2% of each run, Pallas kernels for 0% -> 0%
where the time goes in v1:
time: 155 us
  blocking collectives  56.2 us (36%)
  other arithmetic  51.6 us (33%)
  matrix products  19.9 us (13%)
  between operations  14.4 us (9%)
  local copies, waits for them, and re-layouts  7.38 us (5%)
  waiting for transfers between devices  5.15 us (3%)
    all_gather x2, blocking collectives, loops_treat(): return jnp.sum(jax.lax.all_gather(mat, axis_name=bus_axis), axis=0)  32.9 us
    another operation x7, other arithmetic, orthonormal(): jnp.linalg.cholesky(gram_matrix + shift_value[..., None, None] * identity)  23.9 us
    another operation x5, other arithmetic, orthonormal(): lax.linalg.triangular_solve(lower_factor, flipped(vectors), left_side=Tru...  19.9 us
    all_gather x1, blocking collectives, shards(): lax.all_gather(flat_left, 'col', axis=0, tiled=True)  12.4 us
    all_gather x1, blocking collectives, shards(): lax.all_gather(solved_part, 'col', axis=0, tiled=True)  10.9 us
    dot_general x8, matrix products, stacked_product(): return jnp.matmul(first_matrix, second_matrix, precision=stacked_precision)  7.52 us
    reduce_scatter x1, waiting for transfers between devices, shards(): lax.psum_scatter(jnp.dot(inverse_factor, flat_right, preferred_element_ty...  5.13 us
    another operation x2, matrix products, orthonormal(): lax.linalg.triangular_solve(lower_factor, flipped(vectors), left_side=Tru...  4.75 us
  transfers between devices with their start and end apart: 1, of which 1 were waited for; matrix products, arithmetic and copies ran while one was open for 2% of the time, Pallas kernels for 0%

profile of v1, /device:TPU:0, one launch (start us, length us, event | category | flops | bytes accessed | tf_op | source)
XLA Modules:
  0.0 154.5 jit_solution(4203138791419071987)
XLA Ops:
  7.2 0.0 copy-start
  7.2 0.0 reduce-scatter.2.cloned.1.call-start
  7.2 0.8 iota_compare_fusion.4
  8.0 0.9 broadcast_select_fusion
  9.0 1.5 convolution_bitcast_fusion.1
  10.4 0.0 reduce-scatter.2.cloned.1.call-update
  10.5 0.7 copy-done.17
  11.3 12.4 %all_gather.16 = bf16[2048,128]{0,1:T(8,128)(2,1)S(1)} all-gather(bf16[256,128]{0,1:T(8,128)(2,1)S(1)} %bitcast.193), channel_id=1, replica_groups=mesh['row'=4,'col'=8] {'col'}, dimensions={0}, use_global_device_ids=true | all-gather | bytes 589824 | tf_op jit(solution)/shard_map/all_gather | solution.py:92
  23.7 16.3 %all-gather.1 = bf16[8192,1,32]{0,2,1:T(8,128)(2,1)S(1)} all-gather(bf16[2048,1,32]{0,2,1:T(8,128)(2,1)S(1)} %dynamic-slice_select_fusion), channel_id=3, replica_groups=mesh['row'=4,'col'=8] {'row'}, dimensions={0}, use_global_device_ids=true | all-gather | bytes 655360 | tf_op jit(solution)/shard_map/all_gather | solution.py:15
  40.0 0.4 reshape.198
  40.4 0.1 copy.30
  40.5 1.1 convert.3
  41.6 0.7 reduce_sum.41
  42.3 0.1 iota_compare_fusion.3
  42.4 0.1 fusion.35
  42.5 0.1 broadcast_in_dim.97
  42.6 0.7 copy-done.16
  43.3 1.1 fusion.11
  44.4 0.0 copy-done.9
  44.4 0.3 copy-done.14
  44.7 0.1 bitcast_convert_fusion
  44.8 5.1 %reduce-scatter.2.cloned.1.call-done = f32[256,128]{0,1:T(8,128)} async-done(((f32[2048,128]{0,1:T(8,128)}), f32[256,128]{0,1:T(8,128)}) %reduce-scatter.2.cloned.1.call-update) | async-done | bytes 131088 | tf_op jit(solution)/shard_map/reduce_scatter | solution.py:85
  49.9 0.9 convert_element_type.51
  50.8 10.9 %all_gather.14 = bf16[2048,128]{0,1:T(8,128)(2,1)S(1)} all-gather(bf16[256,128]{0,1:T(8,128)(2,1)S(1)} %convert_element_type.51), channel_id=1, replica_groups=mesh['row'=4,'col'=8] {'col'}, dimensions={0}, use_global_device_ids=true | all-gather | bytes 589824 | tf_op jit(solution)/shard_map/all_gather | solution.py:93
  61.7 0.8 copy-done.13
  62.5 16.6 %all-gather = bf16[8192,1,32]{0,2,1:T(8,128)(2,1)} all-gather(bf16[2048,1,32]{0,2,1:T(8,128)(2,1)S(1)} %dynamic-slice_select_fusion.1), channel_id=2, replica_groups=mesh['row'=4,'col'=8] {'row'}, dimensions={0}, use_global_device_ids=true | all-gather | bytes 655360 | tf_op jit(solution)/shard_map/all_gather | solution.py:15
  79.1 2.2 %reshape.197 = bf16[4,2048,32]{1,0,2:T(4,128)(2,1)} reshape(bf16[8192,1,32]{0,2,1:T(8,128)(2,1)} %all-gather) | data formatting | bytes 1048576 | tf_op jit(solution)/shard_map/all_gather | solution.py:15
  81.4 1.7 %reduce_sum.40 = bf16[2048,32]{0,1:T(8,128)(2,1)S(1)} reduce(bf16[4,2048,32]{1,0,2:T(4,128)(2,1)} %reshape.197, bf16[]{:T(256)} %constant.85.clone.1), dimensions={0}, to_apply=%region_1.2 | reduce | flops 196608 | bytes 655362 | tf_op jit(solution)/shard_map/reduce_sum | solution.py:15
  83.1 1.6 %fusion.38 = f32[32,4,32]{2,0,1:T(8,128)S(1)} fusion(bf16[4,2048,32]{1,2,0:T(8,128)(2,1)} %bitcast.191, bf16[2048,32]{0,1:T(8,128)(2,1)S(1)} %reduce_sum.40), kind=kOutput, calls=%fused_computation.42 | convolution fusion | flops 16777216 | bytes 671744 | tf_op jit(solution)/shard_map/tbr,sbq->tsrq/dot_general | solution.py:112
  84.7 1.6 %fusion.1 = f32[4,1,2048,32]{2,3,0,1:T(8,128)} fusion(bf16[2048,32]{0,1:T(8,128)(2,1)S(1)} %reduce_sum.41, f32[32,4,32]{2,0,1:T(8,128)S(1)} %fusion.38), kind=kOutput, calls=%fused_computation.8 | convolution fusion | flops 100925440 | bytes 1196032 | tf_op jit(solution)/shard_map/dot_general | solution.py:24
  86.3 0.6 fusion.2
  86.9 0.6 fusion.19
  87.5 0.3 copy-done.5
  87.8 1.2 select_reduce_fusion.1
  89.0 0.1 copy.31
  89.1 0.1 fusion.55
  89.2 0.1 copy.32
  89.3 0.1 fusion.42
  89.4 11.9 %custom-call.8 = f32[4,1,32,32]{3,2,1,0:T(8,128)S(1)} custom-call(f32[4,1,32,32]{3,2,1,0:T(8,128)S(1)} %fusion.42), custom_call_target="Cholesky" | custom-call | tf_op jit(solution)/shard_map/jit(cholesky)/cholesky | solution.py:41
  101.3 0.1 compare_reduce_fusion.1
  101.4 0.1 fusion.54
  101.5 9.8 %custom-call.9 = f32[4,1,1,32,32]{3,4,2,1,0:T(8,128)S(1)} custom-call(f32[4,1,1,32,32]{4,3,2,1,0:T(8,128)S(1)} %fusion.54), custom_call_target="InvertDiagBlocksLowerTriangular" | custom-call | tf_op jit(solution)/shard_map/triangular_solve/custom-call.0 | solution.py:42
  111.4 2.4 %convolution_bitcast_fusion = f32[4,2048,32]{1,2,0:T(8,128)S(1)} fusion(f32[4,2048,32]{1,2,0:T(8,128)} %copy-done.2, f32[4,1,1,32,32]{3,4,2,1,0:T(8,128)S(1)} %custom-call.9), kind=kOutput, calls=%fused_computation.6 | convolution fusion | flops 100663296 | bytes 2113536 | tf_op jit(solution)/shard_map/triangular_solve/dot.5 | solution.py:42
  113.8 1.0 fusion.15
  114.8 0.2 copy-done.7
  115.0 0.7 fusion.22
  115.7 0.5 copy-done.10
  116.2 1.0 fusion.9
  117.2 0.2 copy-done.6
  117.4 0.6 fusion.17
  118.1 1.2 select_reduce_fusion
  119.3 0.1 copy.37
  119.4 0.1 fusion.56
  119.4 0.1 copy.38
  119.5 0.1 fusion.40
  119.6 11.7 %custom-call.10 = f32[4,1,32,32]{3,2,1,0:T(8,128)S(1)} custom-call(f32[4,1,32,32]{3,2,1,0:T(8,128)S(1)} %fusion.40), custom_call_target="Cholesky" | custom-call | tf_op jit(solution)/shard_map/jit(cholesky)/cholesky | solution.py:41
  131.4 0.1 compare_reduce_fusion
  131.5 0.1 fusion.49
  131.6 9.8 %custom-call.11 = f32[4,1,1,32,32]{3,4,2,1,0:T(8,128)S(1)} custom-call(f32[4,1,1,32,32]{4,3,2,1,0:T(8,128)S(1)} %fusion.49), custom_call_target="InvertDiagBlocksLowerTriangular" | custom-call | tf_op jit(solution)/shard_map/triangular_solve/custom-call.0 | solution.py:42
  141.4 2.4 %fusion.24 = f32[4,32,2048]{2,1,0:T(8,128)S(1)} fusion(f32[4,2048,32]{1,2,0:T(8,128)} %copy-done.1, f32[4,1,1,32,32]{3,4,2,1,0:T(8,128)S(1)} %custom-call.11), kind=kOutput, calls=%fused_computation.25 | convolution fusion | flops 100663296 | bytes 2113536 | tf_op jit(solution)/shard_map/triangular_solve/dot.5 | solution.py:42
  143.8 1.0 fusion.13
  144.8 1.0 fusion.34
  145.8 0.4 copy-done.8
  146.2 1.4 fusion.4
  (38 shorter events, 0.2 us)
Async XLA Ops:
  7.2 1.8 %copy-start = (bf16[2048,256]{1,0:T(8,128)(2,1)S(1)}, bf16[2048,256]{1,0:T(8,128)(2,1)}, u32[]{:S(2)}) copy-start(bf16[2048,256]{1,0:T(8,128)(2,1)} %param.17) | copy-start | bytes 3145732
  7.2 42.8 %reduce-scatter.2.cloned.1.call-start = ((), (), s32[]{:S(2)}) async-start(), calls=%async_computation.1 | async-start | bytes 1179648 | tf_op jit(solution)/shard_map/reduce_scatter | solution.py:85
  10.4 0.8 copy-start.17
  23.7 18.0 %copy-start.11 = (bf16[2048,128]{0,1:T(8,128)(2,1)}, bf16[2048,128]{0,1:T(8,128)(2,1)S(1)}, u32[]{:S(2)}) copy-start(bf16[2048,128]{0,1:T(8,128)(2,1)S(1)} %all_gather.16) | copy-start | bytes 1572868
  40.5 1.8 %copy-start.18 = (s32[4,1]{0,1:T(1,128)S(1)}, s32[4,1]{0,1:T(1,128)}, u32[]{:S(2)}) copy-start(s32[4,1]{0,1:T(1,128)} %param.13) | copy-start | bytes 52
  40.5 1.9 %copy-start.15 = (bf16[4,1,2048,32]{2,3,1,0:T(8,128)(2,1)S(1)}, bf16[4,1,2048,32]{2,3,1,0:T(8,128)(2,1)}, u32[]{:S(2)}) copy-start(bf16[4,1,2048,32]{2,3,1,0:T(8,128)(2,1)} %param.12) | copy-start | bytes 1572868
  42.4 0.9 copy-start.16
  43.3 1.1 copy-start.9
  43.3 1.4 copy-start.14
  61.7 0.8 copy-start.13
  83.0 3.2 %copy-start.12 = (bf16[2048,128]{0,1:T(8,128)(2,1)S(1)}, bf16[2048,128]{0,1:T(8,128)(2,1)}, u32[]{:S(2)}) copy-start(bf16[2048,128]{0,1:T(8,128)(2,1)} %copy-done.11) | copy-start | bytes 1572868
  86.8 1.0 copy-start.5
  87.8 1.2 copy-start.2
  111.4 2.4 %copy-start.3 = (f32[4,1,2048,32]{2,3,0,1:T(8,128)S(1)}, f32[4,1,2048,32]{2,3,0,1:T(8,128)}, u32[]{:S(2)}) copy-start(f32[4,1,2048,32]{2,3,0,1:T(8,128)} %convert.3) | copy-start | bytes 3145732
  113.7 1.2 copy-start.7
  115.0 1.2 copy-start.10
  116.2 1.2 copy-start.6
  118.1 1.2 copy-start.1
  141.4 2.4 %copy-start.4 = (f32[4,1,2048,32]{2,3,0,1:T(8,128)S(1)}, f32[4,1,2048,32]{2,3,0,1:T(8,128)}, u32[]{:S(2)}) copy-start(f32[4,1,2048,32]{2,3,0,1:T(8,128)} %convert.3) | copy-start | bytes 3145732
  144.8 1.4 copy-start.8
Sparse Core Ops, SparseCore 0:
  11.2 38.7 reduce-scatter.1
